TPU v7x, 32 devices: a whole 2x2x4 slice. The times are simulated.
32 devices in a mesh: section: 2 (over x), dp: 16 (over z, y, core).
Axes of the slice: x: 2, y: 2, z: 4, core: 2. Of those that a mesh axis runs over, the one named last changes fastest.
Arguments:
- edge_data: bfloat16 [2, 2, 1024, 960], P('section', None, 'dp'), may hold values from -6 to 6
- segment_ids: int32 [2, 1024], P(None, 'dp'), may hold values from 0 to 63, as said below
- attn_weight: bfloat16 [2, 960, 2560], P('section', None, 'dp'), may hold values from -0.1875 to 0.1875
- ffn_weight: bfloat16 [2, 3, 960, 2560], P('section', None, None, 'dp'), may hold values from -0.1875 to 0.1875
- gains: bfloat16 [2, 1920], P('section', 'dp'), may hold values from 0.5 to 1.5
Outputs:
- edge_out: bfloat16 [2, 2, 1024, 960], P('section', None, 'dp')
- attention_grad: float32 [2, 960, 2560], P('section', None, 'dp')
- ffn_grad: float32 [2, 3, 960, 2560], P('section', None, None, 'dp')
- gain_grad: float32 [2, 1920], P('section', 'dp')
Inputs may be any that keep to these rules, and one draw needn't show every extreme that they name: `segment_ids`: inside each aligned block of 64 tokens (one index of dp in one micro-batch) the ids start at 0 at the block's first token and rise by 0 or 1 from token to token; tokens of a block with equal ids form one sequence; no sequence crosses a block; some sequence fills a whole block, and some block holds only sequences of one token.
All inputs are finite; a program needn't handle non-finite values.
Results may differ from a plain program's by a relative error of at most 0.02.
Values may be sent and summed in bfloat16 or wider, within the bound.
No kernel may reach another device: no remote copies, remote signals or barrier semaphores. Data moves between devices by JAX's collectives and lax.ppermute only.
A program may use at most 256 MiB of HBM per device.

v0:
```python
import jax
import jax.numpy as jnp
from jax import lax
from jax.sharding import PartitionSpec as P

QUERY_HEADS = 15
KEY_VALUE_HEADS = 5
HEAD_SIZE = 64
epsilon = 1e-05
theta_base = 100000.0
contract_last = (((1,), (1,)), ((), ()))
contract_first = (((0,), (0,)), ((), ()))


def passed_along(array, axis, by):
    length = lax.axis_size(axis)
    pairs = [(i, i + by) for i in range(length) if 0 <= i + by < length]
    return lax.ppermute(array, axis, pairs)


def matmul(left_op, right_op):
    return jnp.dot(left_op, right_op, preferred_element_type=jnp.float32)


def right_trans(left_op, right_op):
    return lax.dot_general(left_op, right_op, contract_last, preferred_element_type=jnp.float32)


def left_trans(left_op, right_op):
    return lax.dot_general(left_op, right_op, contract_first, preferred_element_type=jnp.float32)


def norm_rows(rows, gain):
    return rows * lax.rsqrt(jnp.mean(rows * rows, axis=-1, keepdims=True) + epsilon) * gain


def rotary_apply(rows, cosine_table, sine_values):
    half_size = rows.shape[-1] // 2
    front_part = rows[..., :half_size]
    back_part = rows[..., half_size:]
    return jnp.concatenate(
        [
            front_part * cosine_table - back_part * sine_values,
            back_part * cosine_table + front_part * sine_values,
        ],
        axis=-1,
    )


def block_tables(segments):
    block_len = segments.shape[-1]
    offsets = jnp.arange(block_len, dtype=jnp.int32)
    same_segment = segments[..., :, None] == segments[..., None, :]
    segment_start = jnp.min(jnp.where(same_segment, offsets, block_len), axis=-1)
    positions = (offsets - segment_start).astype(jnp.float32)
    half_size = HEAD_SIZE // 2
    frequency = theta_base ** (-(2.0 * jnp.arange(half_size, dtype=jnp.float32)) / HEAD_SIZE)
    angles = positions[..., None] * frequency
    allowed = same_segment & (offsets[:, None] >= offsets[None, :])
    return (jnp.cos(angles), jnp.sin(angles), allowed)


def attention_scores(query_matrix, key_matrix_rows, allowed):
    scores = jnp.einsum(
        "tgrd,ugd->grtu", query_matrix, key_matrix_rows, preferred_element_type=jnp.float32
    ) * HEAD_SIZE ** (-0.5)
    return jnp.where(allowed, scores, -1000000000.0)


def layer_forward(layer_in, qkv_w, out_w, ffn_w, gain_row, cosine_table, sine_values, allowed):
    sequence_length, model_width = layer_in.shape
    head_column_width = QUERY_HEADS * HEAD_SIZE
    key_value_width = KEY_VALUE_HEADS * HEAD_SIZE
    query_group_count = QUERY_HEADS // KEY_VALUE_HEADS
    residual = layer_in.astype(jnp.float32)
    normed = norm_rows(residual, gain_row[:model_width].astype(jnp.float32)).astype(jnp.bfloat16)
    projected_rows = matmul(normed, qkv_w)
    query_matrix = rotary_apply(
        projected_rows[:, :head_column_width].reshape(
            sequence_length, KEY_VALUE_HEADS, query_group_count, HEAD_SIZE
        ),
        cosine_table[:, None, None, :],
        sine_values[:, None, None, :],
    ).astype(jnp.bfloat16)
    key_matrix_rows = rotary_apply(
        projected_rows[:, head_column_width : head_column_width + key_value_width].reshape(
            sequence_length, KEY_VALUE_HEADS, HEAD_SIZE
        ),
        cosine_table[:, None, :],
        sine_values[:, None, :],
    ).astype(jnp.bfloat16)
    value_matrix_rows = (
        projected_rows[:, head_column_width + key_value_width :]
        .reshape(sequence_length, KEY_VALUE_HEADS, HEAD_SIZE)
        .astype(jnp.bfloat16)
    )
    masked = attention_scores(query_matrix, key_matrix_rows, allowed)
    peak_score = jnp.max(masked, axis=-1, keepdims=True)
    log_total = peak_score + jnp.log(jnp.sum(jnp.exp(masked - peak_score), axis=-1, keepdims=True))
    prob_low = jnp.exp(masked - log_total).astype(jnp.bfloat16)
    attended = jnp.einsum(
        "grtu,ugd->tgrd", prob_low, value_matrix_rows, preferred_element_type=jnp.float32
    )
    attended = attended.reshape(sequence_length, head_column_width).astype(jnp.bfloat16)
    hidden = residual + right_trans(attended, out_w)
    normed_two = norm_rows(hidden, gain_row[model_width:].astype(jnp.float32)).astype(jnp.bfloat16)
    gate_proj = matmul(normed_two, ffn_w[0])
    upward = matmul(normed_two, ffn_w[1])
    active = (jax.nn.silu(gate_proj) * upward).astype(jnp.bfloat16)
    output = hidden + right_trans(active, ffn_w[2])
    saved_state = (
        residual,
        normed,
        query_matrix,
        key_matrix_rows,
        value_matrix_rows,
        log_total,
        attended,
        hidden,
        normed_two,
        gate_proj,
        upward,
        active,
    )
    return (output, saved_state)


def layer_backward(
    grad_out, saved_state, qkv_w, out_w, ffn_w, gain_row, cosine_table, sine_values, allowed
):
    (
        residual,
        normed,
        query_matrix,
        key_matrix_rows,
        value_matrix_rows,
        log_total,
        attended,
        hidden,
        normed_two,
        gate_proj,
        upward,
        active,
    ) = saved_state
    sequence_length, model_width = residual.shape
    head_column_width = QUERY_HEADS * HEAD_SIZE
    key_value_width = KEY_VALUE_HEADS * HEAD_SIZE
    query_group_count = QUERY_HEADS // KEY_VALUE_HEADS
    branch_grad = grad_out.astype(jnp.bfloat16)
    active_grad = matmul(branch_grad, ffn_w[2])
    _, pull_back = jax.vjp(lambda gate_in, up_in: jax.nn.silu(gate_in) * up_in, gate_proj, upward)
    gate_grad, up_grad = pull_back(active_grad)
    gate_grad = gate_grad.astype(jnp.bfloat16)
    up_grad = up_grad.astype(jnp.bfloat16)
    normed_two_grad = right_trans(gate_grad, ffn_w[0]) + right_trans(up_grad, ffn_w[1])
    _, pull_back = jax.vjp(norm_rows, hidden, gain_row[model_width:].astype(jnp.float32))
    hidden_part, gain_two_grad = pull_back(normed_two_grad)
    hidden_grad = grad_out + hidden_part
    mixed_grad = hidden_grad.astype(jnp.bfloat16)
    attended_grad = (
        matmul(mixed_grad, out_w)
        .reshape(sequence_length, KEY_VALUE_HEADS, query_group_count, HEAD_SIZE)
        .astype(jnp.bfloat16)
    )
    prob_full = jnp.exp(attention_scores(query_matrix, key_matrix_rows, allowed) - log_total)
    prob_low = prob_full.astype(jnp.bfloat16)
    value_grad = jnp.einsum(
        "grtu,tgrd->ugd", prob_low, attended_grad, preferred_element_type=jnp.float32
    )
    prob_grad = jnp.einsum(
        "tgrd,ugd->grtu", attended_grad, value_matrix_rows, preferred_element_type=jnp.float32
    )
    scores_grad = (
        prob_full * (prob_grad - jnp.sum(prob_grad * prob_full, axis=-1, keepdims=True))
    ).astype(jnp.bfloat16)
    query_grad = jnp.einsum(
        "grtu,ugd->tgrd", scores_grad, key_matrix_rows, preferred_element_type=jnp.float32
    ) * HEAD_SIZE ** (-0.5)
    key_grad = jnp.einsum(
        "grtu,tgrd->ugd", scores_grad, query_matrix, preferred_element_type=jnp.float32
    ) * HEAD_SIZE ** (-0.5)
    _, pull_back = jax.vjp(
        lambda rows: rotary_apply(
            rows, cosine_table[:, None, None, :], sine_values[:, None, None, :]
        ),
        query_grad,
    )
    (query_grad,) = pull_back(query_grad)
    _, pull_back = jax.vjp(
        lambda rows: rotary_apply(rows, cosine_table[:, None, :], sine_values[:, None, :]), key_grad
    )
    (key_grad,) = pull_back(key_grad)
    qkv_grad = jnp.concatenate(
        [
            query_grad.reshape(sequence_length, head_column_width),
            key_grad.reshape(sequence_length, key_value_width),
            value_grad.reshape(sequence_length, key_value_width),
        ],
        axis=1,
    ).astype(jnp.bfloat16)
    normed_grad = right_trans(qkv_grad, qkv_w)
    _, pull_back = jax.vjp(norm_rows, residual, gain_row[:model_width].astype(jnp.float32))
    input_part, gain_one_grad = pull_back(normed_grad)
    input_grad = hidden_grad + input_part
    pieces = (
        normed,
        qkv_grad,
        mixed_grad,
        attended,
        normed_two,
        gate_grad,
        up_grad,
        branch_grad,
        active,
    )
    return (input_grad, pieces, jnp.concatenate([gain_one_grad, gain_two_grad]))


def owner_rows_maker(piece_group, owners):
    joined = tuple(
        (jnp.concatenate([pieces[member] for pieces in piece_group], axis=0) for member in range(9))
    )
    normed, qkv_grad, mixed_grad, attended, normed_two, gate_grad, up_grad, branch_grad, active = (
        joined
    )
    token_count = normed.shape[0]
    qkv_cols = qkv_grad.shape[1]
    out_cols = attended.shape[1]
    qkv_padded = jnp.concatenate(
        [qkv_grad, jnp.zeros((token_count, out_cols), jnp.bfloat16)], axis=1
    )
    out_padded = jnp.concatenate(
        [jnp.zeros((token_count, qkv_cols), jnp.bfloat16), attended], axis=1
    )
    attn_share = (qkv_cols + out_cols) // owners
    ffn_share = gate_grad.shape[1] // owners
    owner_width = attn_share + 3 * ffn_share

    def one_owner(owner):
        attn_first = lax.dynamic_slice_in_dim(qkv_padded, owner * attn_share, attn_share, 1)
        attn_second = lax.dynamic_slice_in_dim(out_padded, owner * attn_share, attn_share, 1)
        attn_rows = left_trans(attn_first, normed) + left_trans(attn_second, mixed_grad)
        gate_rows = left_trans(
            lax.dynamic_slice_in_dim(gate_grad, owner * ffn_share, ffn_share, 1), normed_two
        )
        up_rows = left_trans(
            lax.dynamic_slice_in_dim(up_grad, owner * ffn_share, ffn_share, 1), normed_two
        )
        down_rows = left_trans(
            lax.dynamic_slice_in_dim(active, owner * ffn_share, ffn_share, 1), branch_grad
        )
        return jnp.concatenate([attn_rows, gate_rows, up_rows, down_rows], axis=0)

    def owner_rows(start, count):
        block_total = count // owner_width
        first_owner = start // owner_width
        owner_list = jnp.arange(block_total, dtype=jnp.int32)
        stacked = lax.map(one_owner, owner_list)
        return stacked.reshape(count, stacked.shape[-1])

    return (owner_rows, owner_width, attn_share, ffn_share)


def unpack_shard(shard, attn_share, ffn_share):
    attention_shard = shard[:attn_share].T[None]
    gate_part = shard[attn_share : attn_share + ffn_share].T
    up_part = shard[attn_share + ffn_share : attn_share + 2 * ffn_share].T
    down_part = shard[attn_share + 2 * ffn_share :].T
    return (attention_shard, jnp.stack([gate_part, up_part, down_part])[None])


def pick_section(leading, first_tree, second_tree):
    return jax.tree.map(
        lambda one_val, two_val: jnp.where(leading, one_val, two_val), first_tree, second_tree
    )


def local(edge_data, segment_ids, attn_weight, ffn_weight, gains):
    micro_count = segment_ids.shape[0]
    owners = lax.axis_size("dp")
    split_at = QUERY_HEADS * HEAD_SIZE + 2 * KEY_VALUE_HEADS * HEAD_SIZE
    leading = lax.axis_index("section") == 0
    table_list = [block_tables(segment_ids[mb_num]) for mb_num in range(micro_count)]
    gathered = (
        lax.all_gather(attn_weight, "dp", axis=2, tiled=True),
        lax.all_gather(ffn_weight, "dp", axis=3, tiled=True),
        lax.all_gather(gains, "dp", axis=1, tiled=True),
    )
    qkv_w = gathered[0][0][:, :split_at]
    out_w = gathered[0][0][:, split_at:]
    ffn_w, gain_row = (gathered[1][0], gathered[2][0])
    received = jnp.zeros_like(edge_data[0, 0])
    saved_list = []
    output_list = []
    for tick_num in range(micro_count + 1):
        own_input = edge_data[0, min(tick_num, micro_count - 1)]
        layer_in = jnp.where(leading, own_input, received)
        cosine_table, sine_values, allowed = pick_section(
            leading, table_list[min(tick_num, micro_count - 1)], table_list[max(tick_num - 1, 0)]
        )
        output, saved_state = layer_forward(
            layer_in, qkv_w, out_w, ffn_w, gain_row, cosine_table, sine_values, allowed
        )
        saved_list.append(saved_state)
        output_list.append(output)
        if tick_num < micro_count:
            received = passed_along(output.astype(jnp.bfloat16), "section", 1)
    back_weights = (
        lax.all_gather(attn_weight, "dp", axis=2, tiled=True),
        lax.all_gather(ffn_weight, "dp", axis=3, tiled=True),
        lax.all_gather(gains, "dp", axis=1, tiled=True),
    )
    qkv_w = back_weights[0][0][:, :split_at]
    out_w = back_weights[0][0][:, split_at:]
    ffn_w, gain_row = (back_weights[1][0], back_weights[2][0])
    grad_received = jnp.zeros_like(edge_data[0, 0])
    piece_list = []
    input_grad_list = []
    gain_total = jnp.zeros(gain_row.shape, jnp.float32)
    for tick_num in range(micro_count + 1):
        saved_state = pick_section(
            leading, saved_list[max(tick_num - 1, 0)], saved_list[min(tick_num + 1, micro_count)]
        )
        cosine_table, sine_values, allowed = pick_section(
            leading, table_list[max(tick_num - 1, 0)], table_list[min(tick_num, micro_count - 1)]
        )
        cotangent = edge_data[1, min(tick_num, micro_count - 1)]
        incoming = jnp.where(leading, grad_received, cotangent).astype(jnp.float32)
        is_valid = jnp.where(leading, tick_num >= 1, tick_num < micro_count)
        incoming = jnp.where(is_valid, incoming, 0.0)
        input_grad, pieces, gain_grad = layer_backward(
            incoming, saved_state, qkv_w, out_w, ffn_w, gain_row, cosine_table, sine_values, allowed
        )
        input_grad_list.append(input_grad)
        gain_total = gain_total + gain_grad
        piece_list.append(pieces)
        if tick_num < micro_count:
            grad_received = passed_along(input_grad.astype(jnp.bfloat16), "section", -1)
    owner_rows, owner_width, attn_share, ffn_share = owner_rows_maker(piece_list, owners)
    total_shard = lax.psum_scatter(
        owner_rows(jnp.int32(0), owner_width * lax.axis_size("dp")),
        "dp",
        scatter_dimension=0,
        tiled=True,
    )
    attention_shard, ffn_shard = unpack_shard(total_shard, attn_share, ffn_share)
    gain_shard = lax.psum_scatter(gain_total[None], "dp", scatter_dimension=1, tiled=True)
    edge_out = jnp.stack(
        [
            jnp.where(leading, input_grad_list[mb_num + 1], output_list[mb_num + 1])
            for mb_num in range(micro_count)
        ]
    ).astype(jnp.bfloat16)
    return (edge_out[None], attention_shard, ffn_shard, gain_shard)


def solution(mesh):
    in_specs = (
        P("section", None, "dp", None),
        P(None, "dp"),
        P("section", None, "dp"),
        P("section", None, None, "dp"),
        P("section", "dp"),
    )
    out_specs = (
        P("section", None, "dp", None),
        P("section", None, "dp"),
        P("section", None, None, "dp"),
        P("section", "dp"),
    )
    return jax.shard_map(local, mesh=mesh, in_specs=in_specs, out_specs=out_specs, check_vma=False)
```

profile of v0, /device:TPU:0, one launch (start us, length us, event | category | flops | bytes accessed | tf_op | source)
XLA Modules:
  0.0 897.1 jit_solution(8501034763040781893)
XLA Ops:
  8.7 1.3 fusion.218
  11.6 35.6 %all-reduce.14 = bf16[1920]{0:T(1024)(128)(2,1)S(1)} all-reduce(bf16[1920]{0:T(1024)(128)(2,1)S(1)} %dynamic-update-slice), channel_id=1, replica_groups=mesh['section'=2,'dp'=16] {'dp'}, use_global_device_ids=true, to_apply=%add.14 | all-reduce | flops 1920 | bytes 7680
  50.9 17.9 %all-gather.5.cloned.1.call-done = bf16[1,960,2560]{1,2,0:T(8,128)(2,1)} async-done(((bf16[1,960,160]{1,2,0:T(8,128)(2,1)}), bf16[1,960,2560]{1,2,0:T(8,128)(2,1)}) %all-gather.5.cloned.1.call-update) | async-done | bytes 4915216 | tf_op jit(solution)/shard_map/all_gather | solution.py:285
  68.8 3.1 fusion.55
  74.4 2.1 multiply_reduce_fusion.23
  76.6 113.0 %all-gather.3.cloned.1.call-done = bf16[1,3,960,2560]{2,3,1,0:T(8,128)(2,1)} async-done(((bf16[1,3,960,160]{2,3,1,0:T(8,128)(2,1)}), bf16[1,3,960,2560]{2,3,1,0:T(8,128)(2,1)}) %all-gather.3.cloned.1.call-update) | async-done | bytes 14745616 | tf_op jit(solution)/shard_map/all_gather | solution.py:310
  189.6 4.2 fusion.41
  193.8 5.3 multiply_convert_fusion.5
  199.1 3.6 fusion.92
  202.7 3.8 collective-permute-start
  210.0 3.1 fusion.53
  215.9 2.3 multiply_reduce_fusion.21
  219.0 4.3 fusion.40
  223.4 5.4 broadcast_select_fusion.2
  228.8 4.6 fusion.112
  234.6 1.7 multiply_reduce_fusion.7
  237.1 2.3 convolution_convert_fusion.5
  243.0 3.9 fusion.90
  247.0 4.4 collective-permute-start.2
  251.4 2.5 collective-permute-done.2
  253.9 4.1 multiply_reduce_fusion.8
  263.1 2.9 multiply_reduce_fusion.16
  268.5 1.7 fusion.136
  270.3 1.3 collective-permute-start.1
  273.7 4.3 fusion.38
  278.1 4.6 broadcast_select_fusion.1
  286.1 4.3 fusion.91
  291.0 1.7 broadcast_select_fusion.19
  292.7 4.5 fusion.115
  298.4 1.7 multiply_reduce_fusion.5
  300.8 2.3 convolution_convert_fusion.4
  309.7 3.4 multiply_reduce_fusion.6
  314.2 1.5 collective-permute-start.3
  317.3 4.3 collective-permute-done.3
  321.7 4.7 fusion.118
  326.5 3.8 fusion.30
  330.3 4.2 multiply_reduce_fusion.3
  335.4 2.3 convolution_convert_fusion.3
  339.8 2.4 pad_maximum_fusion
  345.0 5.3 fusion.60
  350.4 2.8 multiply_reduce_fusion.4
  354.6 133.8 %while.10 = (s32[]{:T(128)}, f32[16,640,960]{2,1,0:T(8,128)}, s32[16]{0:T(128)S(1)}, bf16[192,2560]{0,1:T(8,128)(2,1)}, bf16[192,960]{1,0:T(8,128)(2,1)S(1)}, /*...) while((s32[]{:T(128)}, f32[16,640,960]{2,1,0:T(8,128)}, ...), condition=%wide.region_30.31_spmd, body=%wide.region_29.30_spmd.sunk | while | flops 296908800 | bytes 11109091 | solution.py:258
  361.1 1.8 fusion.297
  369.4 1.8 fusion.297
  373.6 1.3 convolution_add_fusion.5
  377.8 1.9 fusion.297
  386.2 1.8 fusion.297
  394.5 1.9 fusion.297
  403.0 1.8 fusion.297
  407.1 1.3 convolution_add_fusion.5
  411.3 1.8 fusion.297
  419.6 1.9 fusion.297
  428.0 1.8 fusion.297
  436.4 1.9 fusion.297
  444.8 1.9 fusion.297
  453.3 1.8 fusion.297
  461.6 1.8 fusion.297
  469.9 1.9 fusion.297
  478.3 1.8 fusion.297
  486.6 1.8 fusion.297
  489.3 30.0 %all-reduce.15 = f32[1,1920]{1,0:T(1,128)S(1)} all-reduce(f32[1,1920]{1,0:T(1,128)S(1)} %fusion.191), channel_id=3, replica_groups=mesh['section'=2,'dp'=16] {'dp'}, use_global_device_ids=true, to_apply=%region_38.39.clone | all-reduce | flops 1920 | bytes 15360
  520.6 365.6 %reduce-scatter.3.cloned.1.call-done = f32[640,960]{1,0:T(8,128)} async-done(((f32[10240,960]{1,0:T(8,128)}), f32[640,960]{1,0:T(8,128)}) %reduce-scatter.3.cloned.1.call-update) | async-done | bytes 2457616 | tf_op jit(solution)/shard_map/reduce_scatter | solution.py:340
  886.2 2.7 slice_bitcast_fusion.37
  888.9 1.4 maximum_bitcast_fusion.1
  (501 shorter events, 143.9 us)
Async XLA Ops:
  7.2 61.7 %all-gather.5.cloned.1.call-start = ((), (), s32[]{:S(2)}) async-start(), calls=%async_computation.2 | async-start | bytes 5570560 | tf_op jit(solution)/shard_map/all_gather | solution.py:285
  7.9 181.7 %all-gather.3.cloned.1.call-start = ((), (), s32[]{:S(2)}) async-start(), calls=%async_computation.1 | async-start | bytes 16711680 | tf_op jit(solution)/shard_map/all_gather | solution.py:310
  8.6 877.5 %reduce-scatter.3.cloned.1.call-start = ((), (), s32[]{:S(2)}) async-start(), calls=%async_computation.3 | async-start | bytes 44564480 | tf_op jit(solution)/shard_map/reduce_scatter | solution.py:340
  49.2 23.0 %copy-start.73 = (f32[64]{0:T(128)}, f32[64]{0:T(128)S(1)}, u32[]{:S(2)}) copy-start(f32[64]{0:T(128)S(1)} %add_rsqrt_fusion.5) | copy-start | bytes 772
  49.3 160.7 %copy-start.58 = (f32[1,960]{1,0:T(1,128)}, f32[1,960]{1,0:T(1,128)S(1)}, u32[]{:S(2)}) copy-start(f32[1,960]{1,0:T(1,128)S(1)} %get-tuple-element.217) | copy-start | bytes 11524
  49.3 223.6 %copy-start.55 = (f32[1,960]{1,0:T(1,128)}, f32[1,960]{1,0:T(1,128)S(1)}, u32[]{:S(2)}) copy-start(f32[1,960]{1,0:T(1,128)S(1)} %get-tuple-element.216) | copy-start | bytes 11524
  50.9 209.6 %copy-start.15 = (f32[64,32]{1,0:T(8,128)}, f32[64,32]{1,0:T(8,128)S(1)}, u32[]{:S(2)}) copy-start(f32[64,32]{1,0:T(8,128)S(1)} %get-tuple-element.224) | copy-start | bytes 24580
  50.9 209.6 %copy-start.18 = (f32[64,32]{1,0:T(8,128)}, f32[64,32]{1,0:T(8,128)S(1)}, u32[]{:S(2)}) copy-start(f32[64,32]{1,0:T(8,128)S(1)} %get-tuple-element.225) | copy-start | bytes 24580
  76.6 141.7 %copy-start.83 = (f32[64]{0:T(128)}, f32[64]{0:T(128)S(1)}, u32[]{:S(2)}) copy-start(f32[64]{0:T(128)S(1)} %add_rsqrt_fusion.4) | copy-start | bytes 772
  193.8 8.9 copy-start.96
  199.1 14.0 %copy-start.101 = (bf16[64,2560]{1,0:T(8,128)(2,1)}, bf16[64,2560]{1,0:T(8,128)(2,1)S(1)}, u32[]{:S(2)}) copy-start(bf16[64,2560]{1,0:T(8,128)(2,1)S(1)} %get-tuple-element.238) | copy-start | bytes 983044
  202.7 6.5 collective-permute-start
  208.1 31.7 %copy-start.21 = (bf16[64,5,64]{2,0,1:T(8,128)(2,1)}, bf16[64,5,64]{2,0,1:T(8,128)(2,1)S(1)}, u32[]{:S(2)}) copy-start(bf16[64,5,64]{2,0,1:T(8,128)(2,1)S(1)} %copy.141) | copy-start | bytes 122884
  215.9 17.6 %slice-start.2 = ((s8[15728640]{0:T(1024)(128)(4,1)}), s8[4194304]{0:T(1024)(128)(4,1)S(1)}, s32[]{:S(2)}) async-start(s8[15728640]{0:T(1024)(128)(4,1)} %bitcast.493), calls=%async_computation.6 | async-start | bytes 8388608
  219.0 9.8 %copy-start.31 = (bf16[64,960]{1,0:T(8,128)(2,1)}, bf16[64,960]{1,0:T(8,128)(2,1)S(1)}, u32[]{:S(2)}) copy-start(bf16[64,960]{1,0:T(8,128)(2,1)S(1)} %get-tuple-element.137) | copy-start | bytes 368644
  219.0 14.5 %slice-start.3 = ((s8[15728640]{0:T(1024)(128)(4,1)}), s8[4194304]{0:T(1024)(128)(4,1)S(1)}, s32[]{:S(2)}) async-start(s8[15728640]{0:T(1024)(128)(4,1)} %bitcast.493), calls=%async_computation.7 | async-start | bytes 8388608
  223.4 10.1 %copy-start.99 = (f32[64,2560]{1,0:T(8,128)}, f32[64,2560]{1,0:T(8,128)S(1)}, u32[]{:S(2)}) copy-start(f32[64,2560]{1,0:T(8,128)S(1)} %fusion.40) | copy-start | bytes 1966084
  223.4 10.1 %slice-start.4 = ((s8[15728640]{0:T(1024)(128)(4,1)}), s8[4194304]{0:T(1024)(128)(4,1)S(1)}, s32[]{:S(2)}) async-start(s8[15728640]{0:T(1024)(128)(4,1)} %bitcast.493), calls=%async_computation.8 | async-start | bytes 8388608
  241.2 12.7 %copy-start.40 = (bf16[5,64,64]{2,1,0:T(8,128)(2,1)}, bf16[5,64,64]{2,1,0:T(8,128)(2,1)S(1)}, u32[]{:S(2)}) copy-start(bf16[5,64,64]{2,1,0:T(8,128)(2,1)S(1)} %fusion.99) | copy-start | bytes 122884
  242.2 9.1 %copy-start.91 = (f32[64]{0:T(128)S(1)}, f32[64]{0:T(128)}, u32[]{:S(2)}) copy-start(f32[64]{0:T(128)} %get-tuple-element.106) | copy-start | bytes 772
  242.2 11.6 %copy-start.59 = (f32[1,960]{1,0:T(1,128)S(1)}, f32[1,960]{1,0:T(1,128)}, u32[]{:S(2)}) copy-start(f32[1,960]{1,0:T(1,128)} %copy-done.58) | copy-start | bytes 11524
  242.6 15.3 %copy-start.13 = (bf16[64,5,3,64]{0,3,2,1:T(8,128)(2,1)}, bf16[64,5,3,64]{0,3,2,1:T(8,128)(2,1)S(1)}, u32[]{:S(2)}) copy-start(bf16[64,5,3,64]{0,3,2,1:T(8,128)(2,1)S(1)} %copy.148) | copy-start | bytes 368644
  243.0 15.0 %copy-start.42 = (bf16[64,5,64]{0,2,1:T(8,128)(2,1)}, bf16[64,5,64]{0,2,1:T(8,128)(2,1)S(1)}, u32[]{:S(2)}) copy-start(bf16[64,5,64]{0,2,1:T(8,128)(2,1)S(1)} %copy.152) | copy-start | bytes 122884
  243.0 15.0 %slice-start = ((s8[5242880]{0:T(1024)(128)(4,1)}), s8[4194304]{0:T(1024)(128)(4,1)S(1)}, s32[]{:S(2)}) async-start(s8[5242880]{0:T(1024)(128)(4,1)} %bitcast.421), calls=%async_computation.4 | async-start | bytes 8388608
  243.0 15.0 %slice-start.1 = ((s8[5242880]{0:T(1024)(128)(4,1)}), s8[1048576]{0:T(1024)(128)(4,1)S(1)}, s32[]{:S(2)}) async-start(s8[5242880]{0:T(1024)(128)(4,1)} %bitcast.421), calls=%async_computation.5 | async-start | bytes 2097152
  247.0 6.9 collective-permute-start.2
  260.4 8.1 copy-start.9
  260.5 44.0 %copy-start.1 = (bf16[64,5,64]{2,0,1:T(8,128)(2,1)}, bf16[64,5,64]{2,0,1:T(8,128)(2,1)S(1)}, u32[]{:S(2)}) copy-start(bf16[64,5,64]{2,0,1:T(8,128)(2,1)S(1)} %pad_maximum_fusion.13) | copy-start | bytes 122884
  260.5 11.8 %copy-start.94 = (f32[64]{0:T(128)S(1)}, f32[64]{0:T(128)}, u32[]{:S(2)}) copy-start(f32[64]{0:T(128)} %get-tuple-element.103) | copy-start | bytes 772
  260.6 12.3 %copy-start.84 = (f32[64]{0:T(128)S(1)}, f32[64]{0:T(128)}, u32[]{:S(2)}) copy-start(f32[64]{0:T(128)} %copy-done.83) | copy-start | bytes 772
  266.0 16.6 %copy-start.7 = (f32[64,960]{1,0:T(8,128)}, f32[64,960]{1,0:T(8,128)S(1)}, u32[]{:S(2)}) copy-start(f32[64,960]{1,0:T(8,128)S(1)} %get-tuple-element.250) | copy-start | bytes 737284
  266.0 24.4 %copy-start.87 = (f32[64]{0:T(128)}, f32[64]{0:T(128)S(1)}, u32[]{:S(2)}) copy-start(f32[64]{0:T(128)S(1)} %get-tuple-element.197) | copy-start | bytes 772
  270.3 20.7 %collective-permute-start.1 = (bf16[64,960]{1,0:T(8,128)(2,1)}, bf16[64,960]{1,0:T(8,128)(2,1)}, u32[]{:S(2)}, u32[]{:S(2)}) collective-permute-start(bf16[64,960]{1,0:T(8,128)(2,1)} %fusion.136), channel_id=1, source_target_pairs={{16,0},{17,1},{18,2},{19,3},{20,4},{21,5},{22,6},{23,7},{24,8},{25... | collective-permute-start | bytes 368648 | tf_op jit(solution)/shard_map/ppermute | solution.py:18
  271.6 28.5 %copy-start.79 = (f32[64]{0:T(128)}, f32[64]{0:T(128)S(1)}, u32[]{:S(2)}) copy-start(f32[64]{0:T(128)S(1)} %fusion.194) | copy-start | bytes 772
  273.7 23.6 %slice-start.6 = ((s8[15728640]{0:T(1024)(128)(4,1)}), s8[4194304]{0:T(1024)(128)(4,1)S(1)}, s32[]{:S(2)}) async-start(s8[15728640]{0:T(1024)(128)(4,1)} %bitcast.495), calls=%async_computation.10 | async-start | bytes 8388608
  278.0 14.7 %copy-start.100 = (f32[64,2560]{1,0:T(8,128)}, f32[64,2560]{1,0:T(8,128)S(1)}, u32[]{:S(2)}) copy-start(f32[64,2560]{1,0:T(8,128)S(1)} %fusion.38) | copy-start | bytes 1966084
  278.1 19.2 %slice-start.7 = ((s8[15728640]{0:T(1024)(128)(4,1)}), s8[4194304]{0:T(1024)(128)(4,1)S(1)}, s32[]{:S(2)}) async-start(s8[15728640]{0:T(1024)(128)(4,1)} %bitcast.495), calls=%async_computation.11 | async-start | bytes 8388608
  282.7 10.0 %copy-start.104 = (f32[64,2560]{1,0:T(8,128)}, f32[64,2560]{1,0:T(8,128)S(1)}, u32[]{:S(2)}) copy-start(f32[64,2560]{1,0:T(8,128)S(1)} %get-tuple-element.251) | copy-start | bytes 1966084
  283.1 7.9 copy-start.60
  283.1 7.9 copy-start.71
  283.1 7.9 copy-start.74
  284.2 8.5 copy-start.98
  284.2 8.5 copy-start.106
  284.2 13.1 %slice-start.8 = ((s8[15728640]{0:T(1024)(128)(4,1)}), s8[4194304]{0:T(1024)(128)(4,1)S(1)}, s32[]{:S(2)}) async-start(s8[15728640]{0:T(1024)(128)(4,1)} %bitcast.495), calls=%async_computation.12 | async-start | bytes 8388608
  305.3 8.9 copy-start.41
  305.3 7.8 copy-start.4
  305.4 7.8 copy-start.12
  306.5 9.2 %copy-start.92 = (f32[64]{0:T(128)S(1)}, f32[64]{0:T(128)}, u32[]{:S(2)}) copy-start(f32[64]{0:T(128)} %get-tuple-element.104) | copy-start | bytes 772
  309.7 12.0 %copy-start.43 = (bf16[64,5,64]{0,2,1:T(8,128)(2,1)}, bf16[64,5,64]{0,2,1:T(8,128)(2,1)S(1)}, u32[]{:S(2)}) copy-start(bf16[64,5,64]{0,2,1:T(8,128)(2,1)S(1)} %copy.173) | copy-start | bytes 122884
  314.2 7.4 collective-permute-start.3
  326.4 8.1 copy-start.50
  326.4 8.1 copy-start.52
  326.5 8.1 copy-start.88
  330.3 8.0 copy-start.2
  339.8 10.6 %copy-start.5 = (bf16[64,960]{1,0:T(8,128)(2,1)S(1)}, bf16[64,960]{1,0:T(8,128)(2,1)}, u32[]{:S(2)}) copy-start(bf16[64,960]{1,0:T(8,128)(2,1)} %copy-done.3) | copy-start | bytes 368644
  339.8 10.6 %copy-start.62 = (f32[1,960]{1,0:T(1,128)S(1)}, f32[1,960]{1,0:T(1,128)}, u32[]{:S(2)}) copy-start(f32[1,960]{1,0:T(1,128)} %copy-done.58) | copy-start | bytes 11524
  339.8 10.6 %copy-start.89 = (f32[64]{0:T(128)S(1)}, f32[64]{0:T(128)}, u32[]{:S(2)}) copy-start(f32[64]{0:T(128)} %fusion.197) | copy-start | bytes 772
  342.6 10.7 %copy-start.93 = (f32[64]{0:T(128)S(1)}, f32[64]{0:T(128)}, u32[]{:S(2)}) copy-start(f32[64]{0:T(128)} %get-tuple-element.104) | copy-start | bytes 772
  342.6 10.7 %copy-start.72 = (f32[64]{0:T(128)S(1)}, f32[64]{0:T(128)}, u32[]{:S(2)}) copy-start(f32[64]{0:T(128)} %copy-done.70) | copy-start | bytes 772
  342.6 10.7 %copy-start.78 = (f32[64]{0:T(128)S(1)}, f32[64]{0:T(128)}, u32[]{:S(2)}) copy-start(f32[64]{0:T(128)} %copy-done.76) | copy-start | bytes 772
  343.5 9.8 %copy-start.10 = (f32[64,960]{1,0:T(8,128)S(1)}, f32[64,960]{1,0:T(8,128)}, u32[]{:S(2)}) copy-start(f32[64,960]{1,0:T(8,128)} %get-tuple-element.145) | copy-start | bytes 737284
  343.5 10.0 %copy-start.28 = (bf16[64,960]{1,0:T(8,128)(2,1)S(1)}, bf16[64,960]{1,0:T(8,128)(2,1)}, u32[]{:S(2)}) copy-start(bf16[64,960]{1,0:T(8,128)(2,1)} %bitcast_convert_fusion) | copy-start | bytes 368644
  343.5 10.0 %copy-start.30 = (bf16[64,960]{1,0:T(8,128)(2,1)S(1)}, bf16[64,960]{1,0:T(8,128)(2,1)}, u32[]{:S(2)}) copy-start(bf16[64,960]{1,0:T(8,128)(2,1)} %copy-done.29) | copy-start | bytes 368644
  488.4 31.4 %copy-start.39 = (bf16[1,1,64,960]{3,2,1,0:T(8,128)(2,1)S(1)}, bf16[1,1,64,960]{3,2,1,0:T(8,128)(2,1)}, u32[]{:S(2)}) copy-start(bf16[1,1,64,960]{3,2,1,0:T(8,128)(2,1)} %get-tuple-element.140) | copy-start | bytes 368644
  (60 other events, 261.1 us)
Sparse Core Ops, SparseCore 0:
  10.3 58.5 all-gather.4
  71.1 118.4 all-gather.2
  488.6 397.5 reduce-scatter.2
where the time goes:
time: 905 us; the launch traced here: 897 us
  waiting for transfers between devices  506 us (56%)
  matrix products  192 us (21%)
  other arithmetic  67 us (7%)
  blocking collectives  65.5 us (7%)
  local copies, waits for them, and re-layouts  27.3 us (3%)
  between operations  17.5 us (2%)
  loops' own time  11.2 us (1%)
  starting transfers between devices  11.1 us (1%)
    reduce_scatter x1, waiting for transfers between devices, local(): lax.psum_scatter(owner_rows(jnp.int32(0), owner_width * lax.axis_size('dp...  366 us
    all_gather x1, waiting for transfers between devices, local(): lax.all_gather(ffn_weight, 'dp', axis=3, tiled=True)  113 us
    dot_general x80, matrix products, left_trans(): lax.dot_general(left_op, right_op, contract_first, preferred_element_type...  83.9 us
    unnamed x2, blocking collectives  65.5 us
    dot_general x15, matrix products, matmul(): return jnp.dot(left_op, right_op, preferred_element_type=jnp.float32)  56.2 us
    dot_general x15, matrix products, right_trans(): lax.dot_general(left_op, right_op, contract_last, preferred_element_type=...  43 us
    dynamic_update_slice x16, other arithmetic, owner_rows(): stacked = lax.map(one_owner, owner_list)  29.5 us
  transfers between devices with their start and end apart: 7, of which 6 were waited for; matrix products, arithmetic and copies ran while one was open for 4% of the time, Pallas kernels for 0%

commit v1 on v0

--- a/solution.py
+++ b/solution.py
@@ -10,6 +10,30 @@
 theta_base = 100000.0
 contract_last = (((1,), (1,)), ((), ()))
 contract_first = (((0,), (0,)), ((), ()))
+
+
+def series_register(incoming_x):
+    passed = lax.axis_size("dp")
+    reached, current_arr, tile_out = (passed, lax.axis_index("dp"), incoming_x.shape[3])
+    chunks = [(rr, (rr + 1) % reached) for rr in range(reached)]
+    spare = jnp.zeros(
+        (*incoming_x.shape[:3], reached * tile_out, *incoming_x.shape[4:]), incoming_x.dtype
+    )
+    spare = lax.dynamic_update_slice_in_dim(spare, incoming_x, current_arr * tile_out, axis=3)
+    grid = [(rr, (rr - 1) % reached) for rr in range(reached)]
+    extra = reached // 2
+    outer = work_now = incoming_x
+    for t in [*range(1, extra + 1)]:
+        outer = lax.ppermute(outer, "dp", chunks)
+        spare = lax.dynamic_update_slice_in_dim(
+            spare, outer, (current_arr - t) % reached * tile_out, axis=3
+        )
+        if t < reached - extra:
+            work_now = lax.ppermute(work_now, "dp", grid)
+            spare = lax.dynamic_update_slice_in_dim(
+                spare, work_now, (current_arr + t) % reached * tile_out, axis=3
+            )
+    return spare
 
 
 def passed_along(array, axis, by):
@@ -307,7 +331,7 @@
             received = passed_along(output.astype(jnp.bfloat16), "section", 1)
     back_weights = (
         lax.all_gather(attn_weight, "dp", axis=2, tiled=True),
-        lax.all_gather(ffn_weight, "dp", axis=3, tiled=True),
+        series_register(ffn_weight),
         lax.all_gather(gains, "dp", axis=1, tiled=True),
     )
     qkv_w = back_weights[0][0][:, :split_at]

time: 905 us -> 1030 us (1.14)
  starting transfers between devices: 11.1 us -> 113 us
  local copies, waits for them, and re-layouts: 27.3 us -> 62.8 us
  waiting for transfers between devices: 506 us -> 478 us
    all_gather x1, waiting for transfers between devices: 113 us -> 0.02 us  [local(): lax.all_gather(ffn_weight, 'dp', axis=3, tiled=True)]
    ppermute x0 -> x15, waiting for transfers between devices: none -> 101 us  [the longest x8 56 us: series_register(): outer = lax.ppermute(outer, 'dp', chunks)]
    ppermute x0 -> x15, starting transfers between devices: none -> 101 us  [the longest x8 81.9 us: series_register(): outer = lax.ppermute(outer, 'dp', chunks)]
    dynamic_update_slice x0 -> x16, local copies, waits for them, and re-layouts: none -> 22.5 us  [the longest x8 11.9 us: series_register(): lax.dynamic_update_slice_in_dim(spare, outer, (current_arr - t) % reached...]
    all_gather x1, waiting for transfers between devices: 17.9 us -> 0.01 us  [local(): lax.all_gather(attn_weight, 'dp', axis=2, tiled=True)]
  transfers between devices with their start and end apart: 7 -> 22, of which waited for: 6 -> 11; matrix products, arithmetic and copies ran while one was open for 4% -> 8% of each run, Pallas kernels for 0% -> 0%
where the time goes in v1:
time: 1030 us; the launch traced here: 1020 us
  waiting for transfers between devices  478 us (46%)
  matrix products  199 us (19%)
  starting transfers between devices  113 us (11%)
  other arithmetic  70.1 us (7%)
  blocking collectives  64.9 us (6%)
  local copies, waits for them, and re-layouts  62.8 us (6%)
  between operations  17.7 us (2%)
  loops' own time  11.2 us (1%)
    reduce_scatter x1, waiting for transfers between devices, local(): lax.psum_scatter(owner_rows(jnp.int32(0), owner_width * lax.axis_size('dp...  368 us
    dot_general x80, matrix products, left_trans(): lax.dot_general(left_op, right_op, contract_first, preferred_element_type...  83.9 us
    ppermute x8, starting transfers between devices, series_register(): outer = lax.ppermute(outer, 'dp', chunks)  81.9 us
    unnamed x2, blocking collectives  64.9 us
    ppermute x8, waiting for transfers between devices, series_register(): outer = lax.ppermute(outer, 'dp', chunks)  56 us
    dot_general x15, matrix products, matmul(): return jnp.dot(left_op, right_op, preferred_element_type=jnp.float32)  53.5 us
    dot_general x15, matrix products, right_trans(): lax.dot_general(left_op, right_op, contract_last, preferred_element_type=...  53 us
    ppermute x7, waiting for transfers between devices, series_register(): work_now = lax.ppermute(work_now, 'dp', grid)  45.1 us
  transfers between devices with their start and end apart: 22, of which 11 were waited for; matrix products, arithmetic and copies ran while one was open for 8% of the time, Pallas kernels for 0%

profile of v1, /device:TPU:0, one launch (start us, length us, event | category | flops | bytes accessed | tf_op | source)
XLA Modules:
  0.0 1016.4 jit_solution(14970435185553513047)
XLA Ops:
  9.2 5.0 collective-permute-start.1
  14.3 12.2 %collective-permute-done = bf16[1,3,960,160]{2,3,1,0:T(8,128)(2,1)} collective-permute-done((bf16[1,3,960,160]{2,3,1,0:T(8,128)(2,1)}, bf16[1,3,960,160]{2,3,1,0:T(8,128)(2,1)}, u32[]{:S(2)}, u32[]{:S(2)}) %collective-permute-start) | collective-permute-done | bytes 921632 | tf_op jit(solution)/shard_map/ppermute | solution.py:27
  26.5 10.7 %collective-permute-start.2 = (bf16[1,3,960,160]{2,3,1,0:T(8,128)(2,1)}, bf16[1,3,960,160]{2,3,1,0:T(8,128)(2,1)S(1)}, u32[]{:S(2)}, u32[]{:S(2)}) collective-permute-start(bf16[1,3,960,160]{2,3,1,0:T(8,128)(2,1)} %collective-permute-done), channel_id=1, source_target_pairs={{0,1},{1,2},{2,3},{3,4},{4,5},{5,6},{6,7},{7,8},{8,9},{9,10},{10,1... | collective-permute-start | bytes 2764808 | tf_op jit(solution)/shard_map/ppermute | solution.py:27
  39.1 9.8 collective-permute-done.2
  48.9 25.8 %collective-permute-start.4 = (bf16[1,3,960,160]{2,3,1,0:T(8,128)(2,1)S(1)}, bf16[1,3,960,160]{2,3,1,0:T(8,128)(2,1)}, u32[]{:S(2)}, u32[]{:S(2)}) collective-permute-start(bf16[1,3,960,160]{2,3,1,0:T(8,128)(2,1)S(1)} %collective-permute-done.2), channel_id=1, source_target_pairs={{0,1},{1,2},{2,3},{3,4},{4,5},{5,6},{6,7},{7,8},{8,9},{9,10},{10,1... | collective-permute-start | bytes 2764808 | tf_op jit(solution)/shard_map/ppermute | solution.py:27
  77.6 33.4 %all-reduce.14 = bf16[1920]{0:T(1024)(128)(2,1)S(1)} all-reduce(bf16[1920]{0:T(1024)(128)(2,1)S(1)} %dynamic-update-slice), channel_id=1, replica_groups=mesh['section'=2,'dp'=16] {'dp'}, use_global_device_ids=true, to_apply=%add.14 | all-reduce | flops 1920 | bytes 7680
  114.1 29.9 %collective-permute-done.5 = bf16[1,3,960,160]{2,3,1,0:T(8,128)(2,1)} collective-permute-done((bf16[1,3,960,160]{2,3,1,0:T(8,128)(2,1)S(1)}, bf16[1,3,960,160]{2,3,1,0:T(8,128)(2,1)}, u32[]{:S(2)}, u32[]{:S(2)}) %collective-permute-start.5) | collective-permute-done | bytes 921632 | tf_op jit(solution)/shard_map/ppermute | solution.py:32
  144.0 4.7 collective-permute-start.7
  149.7 7.4 squeeze.84
  158.2 2.3 bitcast_dynamic-update-slice_fusion.14
  160.5 2.9 collective-permute-done.7
  163.5 4.7 collective-permute-start.9
  171.3 24.3 %collective-permute-done.8 = bf16[1,3,960,160]{2,3,1,0:T(8,128)(2,1)S(1)} collective-permute-done((bf16[1,3,960,160]{2,3,1,0:T(8,128)(2,1)}, bf16[1,3,960,160]{2,3,1,0:T(8,128)(2,1)S(1)}, u32[]{:S(2)}, u32[]{:S(2)}) %collective-permute-start.8) | collective-permute-done | bytes 921632 | tf_op jit(solution)/shard_map/ppermute | solution.py:27
  195.6 2.4 collective-permute-start.10
  198.0 2.2 bitcast_dynamic-update-slice_fusion.10
  201.3 4.5 collective-permute-start.11
  205.8 2.2 bitcast_dynamic-update-slice_fusion.9
  208.0 2.2 bitcast_dynamic-update-slice_fusion.8
  210.2 2.2 bitcast_dynamic-update-slice_fusion.7
  212.5 9.7 collective-permute-done.10
  222.2 27.4 %collective-permute-start.12 = (bf16[1,3,960,160]{2,3,1,0:T(8,128)(2,1)S(1)}, bf16[1,3,960,160]{2,3,1,0:T(8,128)(2,1)S(1)}, u32[]{:S(2)}, u32[]{:S(2)}) collective-permute-start(bf16[1,3,960,160]{2,3,1,0:T(8,128)(2,1)S(1)} %collective-permute-done.10), channel_id=1, source_target_pairs={{0,1},{1,2},{2,3},{3,4},{4,5},{5,6},{6,7},{7,8},{8,9},{9,10},{10,1... | collective-permute-start | bytes 2764808 | tf_op jit(solution)/shard_map/ppermute | solution.py:27
  253.6 14.5 %collective-permute-start.14 = (bf16[1,3,960,160]{2,3,1,0:T(8,128)(2,1)S(1)}, bf16[1,3,960,160]{2,3,1,0:T(8,128)(2,1)S(1)}, u32[]{:S(2)}, u32[]{:S(2)}) collective-permute-start(bf16[1,3,960,160]{2,3,1,0:T(8,128)(2,1)S(1)} %collective-permute-done.12), channel_id=1, source_target_pairs={{0,1},{1,2},{2,3},{3,4},{4,5},{5,6},{6,7},{7,8},{8,9},{9,10},{10,1... | collective-permute-start | bytes 2764808 | tf_op jit(solution)/shard_map/ppermute | solution.py:27
  269.1 11.1 %collective-permute-done.13 = bf16[1,3,960,160]{2,3,1,0:T(8,128)(2,1)S(1)} collective-permute-done((bf16[1,3,960,160]{2,3,1,0:T(8,128)(2,1)S(1)}, bf16[1,3,960,160]{2,3,1,0:T(8,128)(2,1)S(1)}, u32[]{:S(2)}, u32[]{:S(2)}) %collective-permute-start.13) | collective-permute-done | bytes 921632 | tf_op jit(solution)/shard_map/ppermute | solution.py:32
  281.3 3.1 fusion.55
  291.3 2.1 multiply_reduce_fusion.23
  293.5 4.2 fusion.23
  297.7 5.3 multiply_convert_fusion.5
  303.0 3.6 fusion.92
  306.7 4.3 collective-permute-start.15
  313.8 3.1 fusion.53
  319.4 2.3 multiply_reduce_fusion.21
  322.5 4.3 fusion.22
  326.9 5.4 broadcast_select_fusion.2
  332.3 4.6 fusion.112
  341.4 2.3 convolution_convert_fusion.5
  347.5 14.9 %fusion.90 = bf16[64,960]{1,0:T(8,128)(2,1)S(1)} fusion(f32[64,960]{1,0:T(8,128)S(1)} %get-tuple-element.242, bf16[64,2560]{1,0:T(8,128)(2,1)} %get-tuple-element.133, bf16[1,3,960,2560]{2,3,1,0:T(8,128)(2,1)} %all-gather.5.cloned.1.call-done), kind=kOutput, calls=%fused_computation.119 | convolution fusion | flops 314695680 | bytes 5939200 | tf_op jit(solution)/shard_map/dot_general | solution.py:50
  362.4 4.9 collective-permute-start.17
  367.4 2.5 collective-permute-done.17
  369.9 4.1 multiply_reduce_fusion.8
  380.6 2.9 multiply_reduce_fusion.16
  391.3 4.3 fusion.21
  395.8 4.6 broadcast_select_fusion.1
  403.7 4.3 fusion.91
  410.4 1.9 fusion.115
  415.7 2.3 convolution_convert_fusion.4
  424.7 2.9 multiply_reduce_fusion.6
  431.2 4.9 collective-permute-done.18
  436.2 4.7 fusion.118
  441.0 3.8 fusion.30
  444.8 3.7 multiply_reduce_fusion.3
  450.1 2.3 convolution_convert_fusion.3
  454.4 2.4 pad_maximum_fusion
  459.6 5.3 fusion.60
  464.9 2.8 multiply_reduce_fusion.4
  469.7 133.9 %while.10 = (s32[]{:T(128)}, f32[16,640,960]{2,1,0:T(8,128)}, s32[16]{0:T(128)S(1)}, bf16[192,2560]{0,1:T(8,128)(2,1)}, bf16[192,960]{1,0:T(8,128)(2,1)S(1)}, /*...) while((s32[]{:T(128)}, f32[16,640,960]{2,1,0:T(8,128)}, ...), condition=%wide.region_30.31_spmd, body=%wide.region_29.30_spmd.sunk | while | flops 296908800 | bytes 11109091 | solution.py:282
  484.6 1.9 fusion.297
  493.0 1.9 fusion.297
  509.7 1.8 fusion.297
  551.5 1.9 fusion.297
  559.9 1.9 fusion.297
  585.0 1.9 fusion.297
  604.4 31.4 %all-reduce.15 = f32[1,1920]{1,0:T(1,128)S(1)} all-reduce(f32[1,1920]{1,0:T(1,128)S(1)} %fusion.191), channel_id=3, replica_groups=mesh['section'=2,'dp'=16] {'dp'}, use_global_device_ids=true, to_apply=%region_38.39.clone | all-reduce | flops 1920 | bytes 15360
  637.2 368.2 %reduce-scatter.3.cloned.1.call-done = f32[640,960]{1,0:T(8,128)} async-done(((f32[10240,960]{1,0:T(8,128)}), f32[640,960]{1,0:T(8,128)}) %reduce-scatter.3.cloned.1.call-update) | async-done | bytes 2457616 | tf_op jit(solution)/shard_map/reduce_scatter | solution.py:364
  1005.4 2.7 slice_bitcast_fusion.40
  (562 shorter events, 198.0 us)
Async XLA Ops:
  7.2 274.1 %all-gather.3.cloned.1.call-start = ((), (), s32[]{:S(2)}) async-start(), calls=%async_computation.1 | async-start | bytes 5570560 | tf_op jit(solution)/shard_map/all_gather | solution.py:309
  7.9 285.6 %all-gather.5.cloned.1.call-start = ((), (), s32[]{:S(2)}) async-start(), calls=%async_computation.2 | async-start | bytes 16711680 | tf_op jit(solution)/shard_map/all_gather | solution.py:310
  8.6 996.7 %reduce-scatter.3.cloned.1.call-start = ((), (), s32[]{:S(2)}) async-start(), calls=%async_computation.3 | async-start | bytes 44564480 | tf_op jit(solution)/shard_map/reduce_scatter | solution.py:364
  8.7 17.8 %collective-permute-start = (bf16[1,3,960,160]{2,3,1,0:T(8,128)(2,1)}, bf16[1,3,960,160]{2,3,1,0:T(8,128)(2,1)}, u32[]{:S(2)}, u32[]{:S(2)}) collective-permute-start(bf16[1,3,960,160]{2,3,1,0:T(8,128)(2,1)} %param.10), channel_id=1, source_target_pairs={{0,1},{1,2},{2,3},{3,4},{4,5},{5,6},{6,7},{7,8},{8,9},{9,10},{10,1... | collective-permute-start | bytes 2764808 | tf_op jit(solution)/shard_map/ppermute | solution.py:27
  9.2 28.0 %collective-permute-start.1 = (bf16[1,3,960,160]{2,3,1,0:T(8,128)(2,1)}, bf16[1,3,960,160]{2,3,1,0:T(8,128)(2,1)S(1)}, u32[]{:S(2)}, u32[]{:S(2)}) collective-permute-start(bf16[1,3,960,160]{2,3,1,0:T(8,128)(2,1)} %param.10), channel_id=1, source_target_pairs={{0,15},{1,0},{2,1},{3,2},{4,3},{5,4},{6,5},{7,6},{8,7},{9,8},{10,9... | collective-permute-start | bytes 2764808 | tf_op jit(solution)/shard_map/ppermute | solution.py:32
  26.5 22.4 %collective-permute-start.2 = (bf16[1,3,960,160]{2,3,1,0:T(8,128)(2,1)}, bf16[1,3,960,160]{2,3,1,0:T(8,128)(2,1)S(1)}, u32[]{:S(2)}, u32[]{:S(2)}) collective-permute-start(bf16[1,3,960,160]{2,3,1,0:T(8,128)(2,1)} %collective-permute-done), channel_id=1, source_target_pairs={{0,1},{1,2},{2,3},{3,4},{4,5},{5,6},{6,7},{7,8},{8,9},{9,10},{10,1... | collective-permute-start | bytes 2764808 | tf_op jit(solution)/shard_map/ppermute | solution.py:27
  37.3 73.8 %collective-permute-start.3 = (bf16[1,3,960,160]{2,3,1,0:T(8,128)(2,1)S(1)}, bf16[1,3,960,160]{2,3,1,0:T(8,128)(2,1)S(1)}, u32[]{:S(2)}, u32[]{:S(2)}) collective-permute-start(bf16[1,3,960,160]{2,3,1,0:T(8,128)(2,1)S(1)} %collective-permute-done.1), channel_id=1, source_target_pairs={{0,15},{1,0},{2,1},{3,2},{4,3},{5,4},{6,5},{7,6},{8,7},{9,8},{10,9... | collective-permute-start | bytes 2764808 | tf_op jit(solution)/shard_map/ppermute | solution.py:32
  38.3 243.0 %copy-start.75 = (f32[64]{0:T(128)}, f32[64]{0:T(128)S(1)}, u32[]{:S(2)}) copy-start(f32[64]{0:T(128)S(1)} %add_rsqrt_fusion.5) | copy-start | bytes 772
  48.9 64.7 %collective-permute-start.4 = (bf16[1,3,960,160]{2,3,1,0:T(8,128)(2,1)S(1)}, bf16[1,3,960,160]{2,3,1,0:T(8,128)(2,1)}, u32[]{:S(2)}, u32[]{:S(2)}) collective-permute-start(bf16[1,3,960,160]{2,3,1,0:T(8,128)(2,1)S(1)} %collective-permute-done.2), channel_id=1, source_target_pairs={{0,1},{1,2},{2,3},{3,4},{4,5},{5,6},{6,7},{7,8},{8,9},{9,10},{10,1... | collective-permute-start | bytes 2764808 | tf_op jit(solution)/shard_map/ppermute | solution.py:27
  111.1 37.7 %copy-start.13 = (bf16[1,3,960,160]{2,3,1,0:T(8,128)(2,1)}, bf16[1,3,960,160]{2,3,1,0:T(8,128)(2,1)S(1)}, u32[]{:S(2)}) copy-start(bf16[1,3,960,160]{2,3,1,0:T(8,128)(2,1)S(1)} %collective-permute-done.3) | copy-start | bytes 2764804
  111.1 32.9 %collective-permute-start.5 = (bf16[1,3,960,160]{2,3,1,0:T(8,128)(2,1)S(1)}, bf16[1,3,960,160]{2,3,1,0:T(8,128)(2,1)}, u32[]{:S(2)}, u32[]{:S(2)}) collective-permute-start(bf16[1,3,960,160]{2,3,1,0:T(8,128)(2,1)S(1)} %collective-permute-done.3), channel_id=1, source_target_pairs={{0,15},{1,0},{2,1},{3,2},{4,3},{5,4},{6,5},{7,6},{8,7},{9,8},{10,9... | collective-permute-start | bytes 2764808 | tf_op jit(solution)/shard_map/ppermute | solution.py:32
  111.2 228.6 %copy-start.60 = (f32[1,960]{1,0:T(1,128)}, f32[1,960]{1,0:T(1,128)S(1)}, u32[]{:S(2)}) copy-start(f32[1,960]{1,0:T(1,128)S(1)} %get-tuple-element.216) | copy-start | bytes 11524
  111.2 262.7 %copy-start.64 = (f32[1,960]{1,0:T(1,128)}, f32[1,960]{1,0:T(1,128)S(1)}, u32[]{:S(2)}) copy-start(f32[1,960]{1,0:T(1,128)S(1)} %get-tuple-element.217) | copy-start | bytes 11524
  113.6 44.6 %collective-permute-start.6 = (bf16[1,3,960,160]{2,3,1,0:T(8,128)(2,1)}, bf16[1,3,960,160]{2,3,1,0:T(8,128)(2,1)}, u32[]{:S(2)}, u32[]{:S(2)}) collective-permute-start(bf16[1,3,960,160]{2,3,1,0:T(8,128)(2,1)} %collective-permute-done.4), channel_id=1, source_target_pairs={{0,1},{1,2},{2,3},{3,4},{4,5},{5,6},{6,7},{7,8},{8,9},{9,10},{10,1... | collective-permute-start | bytes 2764808 | tf_op jit(solution)/shard_map/ppermute | solution.py:27
  144.0 19.5 %collective-permute-start.7 = (bf16[1,3,960,160]{2,3,1,0:T(8,128)(2,1)}, bf16[1,3,960,160]{2,3,1,0:T(8,128)(2,1)}, u32[]{:S(2)}, u32[]{:S(2)}) collective-permute-start(bf16[1,3,960,160]{2,3,1,0:T(8,128)(2,1)} %collective-permute-done.5), channel_id=1, source_target_pairs={{0,15},{1,0},{2,1},{3,2},{4,3},{5,4},{6,5},{7,6},{8,7},{9,8},{10,9... | collective-permute-start | bytes 2764808 | tf_op jit(solution)/shard_map/ppermute | solution.py:32
  149.7 227.2 %copy-start.17 = (f32[64,32]{1,0:T(8,128)}, f32[64,32]{1,0:T(8,128)S(1)}, u32[]{:S(2)}) copy-start(f32[64,32]{1,0:T(8,128)S(1)} %get-tuple-element.224) | copy-start | bytes 24580
  149.7 227.2 %copy-start.19 = (f32[64,32]{1,0:T(8,128)}, f32[64,32]{1,0:T(8,128)S(1)}, u32[]{:S(2)}) copy-start(f32[64,32]{1,0:T(8,128)S(1)} %get-tuple-element.225) | copy-start | bytes 24580
  157.2 13.1 %copy-start.14 = (bf16[1,3,960,160]{2,3,1,0:T(8,128)(2,1)S(1)}, bf16[1,3,960,160]{2,3,1,0:T(8,128)(2,1)}, u32[]{:S(2)}) copy-start(bf16[1,3,960,160]{2,3,1,0:T(8,128)(2,1)} %copy-done.13) | copy-start | bytes 2764804
  158.2 37.4 %collective-permute-start.8 = (bf16[1,3,960,160]{2,3,1,0:T(8,128)(2,1)}, bf16[1,3,960,160]{2,3,1,0:T(8,128)(2,1)S(1)}, u32[]{:S(2)}, u32[]{:S(2)}) collective-permute-start(bf16[1,3,960,160]{2,3,1,0:T(8,128)(2,1)} %collective-permute-done.6), channel_id=1, source_target_pairs={{0,1},{1,2},{2,3},{3,4},{4,5},{5,6},{6,7},{7,8},{8,9},{9,10},{10,1... | collective-permute-start | bytes 2764808 | tf_op jit(solution)/shard_map/ppermute | solution.py:27
  163.5 37.9 %collective-permute-start.9 = (bf16[1,3,960,160]{2,3,1,0:T(8,128)(2,1)}, bf16[1,3,960,160]{2,3,1,0:T(8,128)(2,1)S(1)}, u32[]{:S(2)}, u32[]{:S(2)}) collective-permute-start(bf16[1,3,960,160]{2,3,1,0:T(8,128)(2,1)} %collective-permute-done.7), channel_id=1, source_target_pairs={{0,15},{1,0},{2,1},{3,2},{4,3},{5,4},{6,5},{7,6},{8,7},{9,8},{10,9... | collective-permute-start | bytes 2764808 | tf_op jit(solution)/shard_map/ppermute | solution.py:32
  195.6 26.6 %collective-permute-start.10 = (bf16[1,3,960,160]{2,3,1,0:T(8,128)(2,1)S(1)}, bf16[1,3,960,160]{2,3,1,0:T(8,128)(2,1)S(1)}, u32[]{:S(2)}, u32[]{:S(2)}) collective-permute-start(bf16[1,3,960,160]{2,3,1,0:T(8,128)(2,1)S(1)} %collective-permute-done.8), channel_id=1, source_target_pairs={{0,1},{1,2},{2,3},{3,4},{4,5},{5,6},{6,7},{7,8},{8,9},{9,10},{10,1... | collective-permute-start | bytes 2764808 | tf_op jit(solution)/shard_map/ppermute | solution.py:27
  201.3 49.2 %collective-permute-start.11 = (bf16[1,3,960,160]{2,3,1,0:T(8,128)(2,1)S(1)}, bf16[1,3,960,160]{2,3,1,0:T(8,128)(2,1)S(1)}, u32[]{:S(2)}, u32[]{:S(2)}) collective-permute-start(bf16[1,3,960,160]{2,3,1,0:T(8,128)(2,1)S(1)} %collective-permute-done.9), channel_id=1, source_target_pairs={{0,15},{1,0},{2,1},{3,2},{4,3},{5,4},{6,5},{7,6},{8,7},{9,8},{10,9... | collective-permute-start | bytes 2764808 | tf_op jit(solution)/shard_map/ppermute | solution.py:32
  222.2 31.4 %collective-permute-start.12 = (bf16[1,3,960,160]{2,3,1,0:T(8,128)(2,1)S(1)}, bf16[1,3,960,160]{2,3,1,0:T(8,128)(2,1)S(1)}, u32[]{:S(2)}, u32[]{:S(2)}) collective-permute-start(bf16[1,3,960,160]{2,3,1,0:T(8,128)(2,1)S(1)} %collective-permute-done.10), channel_id=1, source_target_pairs={{0,1},{1,2},{2,3},{3,4},{4,5},{5,6},{6,7},{7,8},{8,9},{9,10},{10,1... | collective-permute-start | bytes 2764808 | tf_op jit(solution)/shard_map/ppermute | solution.py:27
  250.5 30.8 %copy-start = (bf16[1,2,64,960]{3,2,1,0:T(8,128)(2,1)S(1)}, bf16[1,2,64,960]{3,2,1,0:T(8,128)(2,1)}, u32[]{:S(2)}) copy-start(bf16[1,2,64,960]{3,2,1,0:T(8,128)(2,1)} %param.7) | copy-start | bytes 737284
  250.5 29.7 %collective-permute-start.13 = (bf16[1,3,960,160]{2,3,1,0:T(8,128)(2,1)S(1)}, bf16[1,3,960,160]{2,3,1,0:T(8,128)(2,1)S(1)}, u32[]{:S(2)}, u32[]{:S(2)}) collective-permute-start(bf16[1,3,960,160]{2,3,1,0:T(8,128)(2,1)S(1)} %collective-permute-done.11), channel_id=1, source_target_pairs={{0,15},{1,0},{2,1},{3,2},{4,3},{5,4},{6,5},{7,6},{8,7},{9,8},{10,9... | collective-permute-start | bytes 2764808 | tf_op jit(solution)/shard_map/ppermute | solution.py:32
  253.6 57.3 %collective-permute-start.14 = (bf16[1,3,960,160]{2,3,1,0:T(8,128)(2,1)S(1)}, bf16[1,3,960,160]{2,3,1,0:T(8,128)(2,1)S(1)}, u32[]{:S(2)}, u32[]{:S(2)}) collective-permute-start(bf16[1,3,960,160]{2,3,1,0:T(8,128)(2,1)S(1)} %collective-permute-done.12), channel_id=1, source_target_pairs={{0,1},{1,2},{2,3},{3,4},{4,5},{5,6},{6,7},{7,8},{8,9},{9,10},{10,1... | collective-permute-start | bytes 2764808 | tf_op jit(solution)/shard_map/ppermute | solution.py:27
  306.7 6.3 collective-permute-start.15
  312.9 31.4 %copy-start.23 = (bf16[64,5,64]{2,0,1:T(8,128)(2,1)}, bf16[64,5,64]{2,0,1:T(8,128)(2,1)S(1)}, u32[]{:S(2)}) copy-start(bf16[64,5,64]{2,0,1:T(8,128)(2,1)S(1)} %copy.141) | copy-start | bytes 122884
  319.4 17.6 %slice-start = ((s8[15728640]{0:T(1024)(128)(4,1)}), s8[4194304]{0:T(1024)(128)(4,1)S(1)}, s32[]{:S(2)}) async-start(s8[15728640]{0:T(1024)(128)(4,1)} %bitcast.448), calls=%async_computation.4 | async-start | bytes 8388608
  322.5 14.5 %slice-start.1 = ((s8[15728640]{0:T(1024)(128)(4,1)}), s8[4194304]{0:T(1024)(128)(4,1)S(1)}, s32[]{:S(2)}) async-start(s8[15728640]{0:T(1024)(128)(4,1)} %bitcast.448), calls=%async_computation.5 | async-start | bytes 8388608
  326.8 10.1 copy-start.106
  326.9 10.1 slice-start.2
  345.7 24.2 %copy-start.43 = (bf16[5,64,64]{2,1,0:T(8,128)(2,1)}, bf16[5,64,64]{2,1,0:T(8,128)(2,1)S(1)}, u32[]{:S(2)}) copy-start(bf16[5,64,64]{2,1,0:T(8,128)(2,1)S(1)} %fusion.99) | copy-start | bytes 122884
  346.8 20.6 %copy-start.98 = (f32[64]{0:T(128)S(1)}, f32[64]{0:T(128)}, u32[]{:S(2)}) copy-start(f32[64]{0:T(128)} %get-tuple-element.106) | copy-start | bytes 772
  347.1 26.8 %copy-start.15 = (bf16[64,5,3,64]{0,3,2,1:T(8,128)(2,1)}, bf16[64,5,3,64]{0,3,2,1:T(8,128)(2,1)S(1)}, u32[]{:S(2)}) copy-start(bf16[64,5,3,64]{0,3,2,1:T(8,128)(2,1)S(1)} %copy.148) | copy-start | bytes 368644
  347.5 26.4 %copy-start.45 = (bf16[64,5,64]{0,2,1:T(8,128)(2,1)}, bf16[64,5,64]{0,2,1:T(8,128)(2,1)S(1)}, u32[]{:S(2)}) copy-start(bf16[64,5,64]{0,2,1:T(8,128)(2,1)S(1)} %copy.152) | copy-start | bytes 122884
  347.5 26.5 %slice-start.8 = ((s8[5242880]{0:T(1024)(128)(4,1)}), s8[4194304]{0:T(1024)(128)(4,1)S(1)}, s32[]{:S(2)}) async-start(s8[5242880]{0:T(1024)(128)(4,1)} %bitcast.463), calls=%async_computation.12 | async-start | bytes 8388608
  347.5 26.5 %slice-start.9 = ((s8[5242880]{0:T(1024)(128)(4,1)}), s8[1048576]{0:T(1024)(128)(4,1)S(1)}, s32[]{:S(2)}) async-start(s8[5242880]{0:T(1024)(128)(4,1)} %bitcast.463), calls=%async_computation.13 | async-start | bytes 2097152
  362.4 7.4 collective-permute-start.17
  377.1 42.4 %copy-start.2 = (bf16[64,5,64]{2,0,1:T(8,128)(2,1)}, bf16[64,5,64]{2,0,1:T(8,128)(2,1)S(1)}, u32[]{:S(2)}) copy-start(bf16[64,5,64]{2,0,1:T(8,128)(2,1)S(1)} %pad_maximum_fusion.13) | copy-start | bytes 122884
  377.1 12.8 %copy-start.101 = (f32[64]{0:T(128)S(1)}, f32[64]{0:T(128)}, u32[]{:S(2)}) copy-start(f32[64]{0:T(128)} %get-tuple-element.103) | copy-start | bytes 772
  377.1 13.4 %copy-start.61 = (f32[1,960]{1,0:T(1,128)S(1)}, f32[1,960]{1,0:T(1,128)}, u32[]{:S(2)}) copy-start(f32[1,960]{1,0:T(1,128)} %copy-done.60) | copy-start | bytes 11524
  377.2 13.4 %copy-start.90 = (f32[64]{0:T(128)S(1)}, f32[64]{0:T(128)}, u32[]{:S(2)}) copy-start(f32[64]{0:T(128)} %copy-done.88) | copy-start | bytes 772
  383.5 16.8 %copy-start.8 = (f32[64,960]{1,0:T(8,128)}, f32[64,960]{1,0:T(8,128)S(1)}, u32[]{:S(2)}) copy-start(f32[64,960]{1,0:T(8,128)S(1)} %get-tuple-element.250) | copy-start | bytes 737284
  383.5 24.5 %copy-start.93 = (f32[64]{0:T(128)}, f32[64]{0:T(128)S(1)}, u32[]{:S(2)}) copy-start(f32[64]{0:T(128)S(1)} %get-tuple-element.197) | copy-start | bytes 772
  387.9 20.7 %collective-permute-start.16 = (bf16[64,960]{1,0:T(8,128)(2,1)}, bf16[64,960]{1,0:T(8,128)(2,1)}, u32[]{:S(2)}, u32[]{:S(2)}) collective-permute-start(bf16[64,960]{1,0:T(8,128)(2,1)} %fusion.136), channel_id=1, source_target_pairs={{16,0},{17,1},{18,2},{19,3},{20,4},{21,5},{22,6},{23,7},{24,8},{25... | collective-permute-start | bytes 368648 | tf_op jit(solution)/shard_map/ppermute | solution.py:42
  389.2 25.9 %copy-start.84 = (f32[64]{0:T(128)}, f32[64]{0:T(128)S(1)}, u32[]{:S(2)}) copy-start(f32[64]{0:T(128)S(1)} %fusion.194) | copy-start | bytes 772
  391.3 19.0 %slice-start.4 = ((s8[15728640]{0:T(1024)(128)(4,1)}), s8[4194304]{0:T(1024)(128)(4,1)S(1)}, s32[]{:S(2)}) async-start(s8[15728640]{0:T(1024)(128)(4,1)} %bitcast.450), calls=%async_computation.8 | async-start | bytes 8388608
  395.7 14.6 %copy-start.107 = (f32[64,2560]{1,0:T(8,128)}, f32[64,2560]{1,0:T(8,128)S(1)}, u32[]{:S(2)}) copy-start(f32[64,2560]{1,0:T(8,128)S(1)} %fusion.21) | copy-start | bytes 1966084
  395.7 14.6 %slice-start.5 = ((s8[15728640]{0:T(1024)(128)(4,1)}), s8[4194304]{0:T(1024)(128)(4,1)S(1)}, s32[]{:S(2)}) async-start(s8[15728640]{0:T(1024)(128)(4,1)} %bitcast.450), calls=%async_computation.9 | async-start | bytes 8388608
  395.7 14.6 %slice-start.6 = ((s8[15728640]{0:T(1024)(128)(4,1)}), s8[4194304]{0:T(1024)(128)(4,1)S(1)}, s32[]{:S(2)}) async-start(s8[15728640]{0:T(1024)(128)(4,1)} %bitcast.450), calls=%async_computation.10 | async-start | bytes 8388608
  400.3 10.0 copy-start.111
  423.5 17.4 %copy-start.16 = (bf16[64,5,3,64]{0,3,2,1:T(8,128)(2,1)}, bf16[64,5,3,64]{0,3,2,1:T(8,128)(2,1)S(1)}, u32[]{:S(2)}) copy-start(bf16[64,5,3,64]{0,3,2,1:T(8,128)(2,1)S(1)} %copy.169) | copy-start | bytes 368644
  424.6 16.2 %copy-start.46 = (bf16[64,5,64]{0,2,1:T(8,128)(2,1)}, bf16[64,5,64]{0,2,1:T(8,128)(2,1)S(1)}, u32[]{:S(2)}) copy-start(bf16[64,5,64]{0,2,1:T(8,128)(2,1)S(1)} %copy.173) | copy-start | bytes 122884
  428.6 7.5 collective-permute-start.18
  454.4 10.5 %copy-start.6 = (bf16[64,960]{1,0:T(8,128)(2,1)S(1)}, bf16[64,960]{1,0:T(8,128)(2,1)}, u32[]{:S(2)}) copy-start(bf16[64,960]{1,0:T(8,128)(2,1)} %copy-done.4) | copy-start | bytes 368644
  454.4 10.5 %copy-start.67 = (f32[1,960]{1,0:T(1,128)S(1)}, f32[1,960]{1,0:T(1,128)}, u32[]{:S(2)}) copy-start(f32[1,960]{1,0:T(1,128)} %copy-done.64) | copy-start | bytes 11524
  457.1 10.6 %copy-start.100 = (f32[64]{0:T(128)S(1)}, f32[64]{0:T(128)}, u32[]{:S(2)}) copy-start(f32[64]{0:T(128)} %get-tuple-element.104) | copy-start | bytes 772
  457.1 10.6 %copy-start.80 = (f32[64]{0:T(128)S(1)}, f32[64]{0:T(128)}, u32[]{:S(2)}) copy-start(f32[64]{0:T(128)} %copy-done.78) | copy-start | bytes 772
  457.1 10.6 %copy-start.83 = (f32[64]{0:T(128)S(1)}, f32[64]{0:T(128)}, u32[]{:S(2)}) copy-start(f32[64]{0:T(128)} %copy-done.81) | copy-start | bytes 772
  458.0 10.6 %copy-start.30 = (bf16[64,960]{1,0:T(8,128)(2,1)S(1)}, bf16[64,960]{1,0:T(8,128)(2,1)}, u32[]{:S(2)}) copy-start(bf16[64,960]{1,0:T(8,128)(2,1)} %bitcast_convert_fusion) | copy-start | bytes 368644
  458.0 10.6 %copy-start.32 = (bf16[64,960]{1,0:T(8,128)(2,1)S(1)}, bf16[64,960]{1,0:T(8,128)(2,1)}, u32[]{:S(2)}) copy-start(bf16[64,960]{1,0:T(8,128)(2,1)} %copy-done.31) | copy-start | bytes 368644
  603.6 32.9 %copy-start.35 = (bf16[1,1,64,960]{3,2,1,0:T(8,128)(2,1)S(1)}, bf16[1,1,64,960]{3,2,1,0:T(8,128)(2,1)}, u32[]{:S(2)}) copy-start(bf16[1,1,64,960]{3,2,1,0:T(8,128)(2,1)} %get-tuple-element.194) | copy-start | bytes 368644
  603.6 32.9 %copy-start.42 = (bf16[1,1,64,960]{3,2,1,0:T(8,128)(2,1)S(1)}, bf16[1,1,64,960]{3,2,1,0:T(8,128)(2,1)}, u32[]{:S(2)}) copy-start(bf16[1,1,64,960]{3,2,1,0:T(8,128)(2,1)} %get-tuple-element.140) | copy-start | bytes 368644
  (82 other events, 460.0 us)
Sparse Core Ops, SparseCore 0:
  10.3 86.2 all-gather.2
  98.8 186.1 all-gather.4
  603.7 401.5 reduce-scatter.2
